TPU v7x, 32 devices: a whole 2x2x4 slice. The times are simulated.
32 devices in a mesh: sector: 4 (over x, core), op: 8 (over z, y).
Axes of the slice: x: 2, y: 2, z: 4, core: 2. Of those that a mesh axis runs over, the one named last changes fastest.
Arguments:
- wave: float32 [8, 768, 768], P('sector', 'op'), may hold values from -6 to 6
- onsite: float32 [8, 768, 768], P('sector', 'op'), may hold values from -2 to 2
- left_ops: float32 [8, 16, 768, 768], P('sector', 'op'), may hold values from -0.21875 to 0.21875
- right_ops: float32 [8, 16, 768, 768], P('sector', 'op'), may hold values from -0.0546875 to 0.0546875
- coupling: int32 [8, 16], P('sector', 'op'), may hold values from 0 to 2
Outputs:
- sigma: float32 [8, 768, 768], P('sector', 'op')
- correction: float32 [8, 768, 768], P('sector', 'op')
All inputs are finite; a program needn't handle non-finite values.
Results may differ from a plain program's by a relative error of at most 0.0001.
Values sent between devices are 32-bit elements; how exact they have to be, the bound alone decides.
No kernel may reach another device: no remote copies, remote signals or barrier semaphores. Data moves between devices by JAX's collectives and lax.ppermute only.
A program may use at most 128 MiB of HBM per device.

v0:
```python
import jax
import jax.numpy as jnp
from jax import lax
from jax.sharding import PartitionSpec as P


def shifted(value, axis, by):
    length = lax.axis_size(axis)
    return lax.ppermute(value, axis, [(i, (i + by) % length) for i in range(length)])


def on_device(wave, onsite, left_ops, right_ops, coupling):
    highest = lax.Precision.HIGHEST
    rows = wave.shape[1]
    width = wave.shape[2]
    ahead_rows = shifted(wave[0:1], "sector", -1)
    own_full, ahead_full = (
        lax.all_gather(wave, "op", axis=1, tiled=True),
        lax.all_gather(ahead_rows, "op", axis=1, tiled=True),
    )
    following = jnp.concatenate([own_full[1:2], ahead_full], axis=0)
    left_fwd = jnp.einsum("jkac,jcb->jkab", left_ops, own_full, precision=highest)
    left_back = jnp.einsum("jkca,jcb->jkab", left_ops, following, precision=highest)
    weights = coupling.astype(jnp.float32)[:, :, None, None]
    forward = jnp.einsum("jkab,jkcb->jac", weights * left_fwd, right_ops, precision=highest)
    backward = jnp.einsum("jkab,jkbc->jac", weights * left_back, right_ops, precision=highest)
    partial_sums = jnp.stack([backward[0], backward[1] + forward[0]], axis=0)
    leaving = forward[1:2]
    summed, outgoing = (
        lax.psum_scatter(partial_sums, "op", scatter_dimension=1, tiled=True),
        lax.psum_scatter(leaving, "op", scatter_dimension=1, tiled=True),
    )
    arriving = shifted(outgoing, "sector", 1)
    sigma = onsite * wave + summed + jnp.concatenate([arriving, jnp.zeros_like(arriving)], axis=0)
    total = wave.shape[0] * rows * width * lax.axis_size("sector") * lax.axis_size("op")
    norm_sq, energy_sum = lax.psum((jnp.sum(wave * wave), jnp.sum(wave * sigma)), ("sector", "op"))
    energy = energy_sum / norm_sq
    gap = onsite - energy
    first = (sigma - energy * wave) * gap / jnp.maximum(gap * gap, 1.0)
    correlation = lax.psum(jnp.sum(wave * first), ("sector", "op"))
    second = first - correlation / norm_sq * wave
    length_sq = lax.psum(jnp.sum(second * second), ("sector", "op"))
    correction = second * lax.rsqrt(length_sq / total + 1e-06)
    return (sigma, correction)


def solution(mesh):
    return jax.shard_map(
        on_device,
        mesh=mesh,
        in_specs=(
            P("sector", "op", None),
            P("sector", "op", None),
            P("sector", "op", None, None),
            P("sector", "op", None, None),
            P("sector", "op"),
        ),
        out_specs=(P("sector", "op", None), P("sector", "op", None)),
        check_vma=False,
    )
```

profile of v0, /device:TPU:0, one launch (start us, length us, event | category | flops | bytes accessed | tf_op | source)
XLA Modules:
  0.0 506.4 jit_solution(11977234330600486002)
XLA Ops:
  7.2 0.0 all-gather.3.cloned.1.call-start
  7.2 0.7 all-gather.3.cloned.1.call-update
  7.9 0.0 all-gather.5.cloned.1.call-start
  7.9 1.0 slice.19
  8.9 2.5 collective-permute-start
  11.4 4.2 collective-permute-done
  15.6 0.0 copy-start.4
  15.6 0.7 copy-done.4
  16.3 0.0 all-gather.5.cloned.1.call-update
  16.4 0.0 reduce-scatter.5.cloned.1.call-start
  16.4 0.7 convert_element_type.3
  17.1 75.2 %all-gather.3.cloned.1.call-done = f32[2,768,768]{2,1,0:T(8,128)} async-done(((f32[2,96,768]{2,1,0:T(8,128)}), f32[2,768,768]{2,1,0:T(8,128)}) %all-gather.3.cloned.1.call-update) | async-done | bytes 4718608 | tf_op jit(solution)/shard_map/all_gather | solution.py:18
  92.3 0.0 copy-start.1
  92.3 0.0 slice-start.3
  92.3 2.3 copy-done.1
  94.6 0.0 slice-start.4
  94.6 0.0 slice-start.5
  94.6 26.4 %fusion.8 = f32[2,2,768,768]{3,2,1,0:T(8,128)S(1)} fusion(f32[2,2,768,768]{3,2,1,0:T(8,128)} %param.7, f32[2,768,768]{2,1,0:T(8,128)S(1)} %copy-done.1), kind=kOutput, calls=%fused_computation.10 | convolution fusion | flops 21743271936 | bytes 23592960 | tf_op jit(solution)/shard_map/jkac,jcb->jkab/dot_general | solution.py:22
  121.0 0.0 slice-done.3
  121.0 0.0 slice-done.4
  121.0 0.0 slice-done.5
  121.0 0.0 slice-start
  121.0 24.9 %fusion.12 = f32[2,768,768]{2,1,0:T(8,128)} fusion(f32[2,2,768,768]{3,2,1,0:T(8,128)S(1)} %bitcast.28, f32[2,2,768,768]{3,2,1,0:T(8,128)S(1)} %fusion.8, f32[2,2]{1,0:T(2,128)S(1)} %convert_element_type.3), kind=kOutput, calls=%fused_computation.15 | convolution fusion | flops 21745631232 | bytes 23592976 | tf_op jit(solution)/shard_map/jkab,jkcb->jac/dot_general | solution.py:25
  146.0 0.0 all-gather.5.cloned.1.call-done
  146.0 0.0 slice-done
  146.0 0.0 slice-start.1
  146.0 29.8 %fusion.5 = f32[2,768,2,768]{1,3,2,0:T(8,128)S(1)} fusion(f32[2,2,768,768]{3,2,1,0:T(8,128)} %param.7, f32[1,768,768]{2,1,0:T(8,128)} %all-gather.5.cloned.1.call-done, f32[1,768,768]{2,1,0:T(8,128)S(1)} %slice-done), kind=kOutput, calls=%fused_computation.6 | convolution fusion | flops 21744451584 | bytes 23592960 | tf_op jit(solution)/shard_map/jkca,jcb->jkab/dot_general | solution.py:23
  175.8 0.0 slice-start.2
  175.8 25.7 %fusion.15 = f32[2,768,768]{2,1,0:T(8,128)S(1)} fusion(f32[2,2,768,768]{3,2,1,0:T(8,128)} %param.8, f32[2,768,2,768]{1,3,2,0:T(8,128)S(1)} %fusion.5, f32[2,2]{1,0:T(2,128)S(1)} %convert_element_type.3), kind=kOutput, calls=%fused_computation.16 | convolution fusion | flops 21745631232 | bytes 23592976 | tf_op jit(solution)/shard_map/jkab,jkbc->jac/dot_general | solution.py:26
  201.5 0.0 slice-done.1
  201.6 0.0 slice-done.2
  201.6 2.8 fusion.19
  204.3 0.0 reduce-scatter.5.cloned.1.call-update
  204.4 0.0 reduce-scatter.3.cloned.1.call-start
  204.4 4.1 pad_maximum_fusion
  208.5 0.0 copy-start
  208.5 0.0 copy-start.2
  208.5 0.0 reduce-scatter.3.cloned.1.call-update
  208.5 63.8 %reduce-scatter.5.cloned.1.call-done = f32[1,96,768]{2,1,0:T(8,128)} async-done(((f32[1,768,768]{2,1,0:T(8,128)}), f32[1,96,768]{2,1,0:T(8,128)}) %reduce-scatter.5.cloned.1.call-update) | async-done | bytes 294928 | tf_op jit(solution)/shard_map/reduce_scatter | solution.py:31
  272.4 0.0 collective-permute-start.1
  272.4 6.4 %collective-permute-done.1 = f32[1,96,768]{2,1,0:T(8,128)S(1)} collective-permute-done((f32[1,96,768]{2,1,0:T(8,128)}, f32[1,96,768]{2,1,0:T(8,128)S(1)}, u32[]{:S(2)}, u32[]{:S(2)}) %collective-permute-start.1) | collective-permute-done | bytes 294944 | tf_op jit(solution)/shard_map/ppermute | solution.py:9
  278.7 92.0 %reduce-scatter.3.cloned.1.call-done = f32[2,96,768]{2,1,0:T(8,128)} async-done(((f32[2,768,768]{2,1,0:T(8,128)}), f32[2,96,768]{2,1,0:T(8,128)}) %reduce-scatter.3.cloned.1.call-update) | async-done | bytes 589840 | tf_op jit(solution)/shard_map/reduce_scatter | solution.py:30
  370.8 0.0 copy-done
  370.8 0.0 copy-done.2
  370.8 1.8 multiply_reduce_fusion.2
  372.6 0.0 copy-start.3
  372.6 40.4 %all-reduce.1 = (f32[]{:T(128)}, f32[]{:T(128)}) all-reduce(f32[]{:T(128)} %get-tuple-element.3, f32[]{:T(128)} %get-tuple-element.2), channel_id=1, replica_groups=mesh['sector'=4,'op'=8] {'sector','op'}, use_global_device_ids=true, to_apply=%region_3.0 | all-reduce | flops 2 | bytes 16 | tf_op jit(solution)/shard_map/psum | solution.py:36
  414.4 0.8 multiply_reduce_fusion.1
  415.2 39.3 %psum.30 = f32[]{:T(128)} all-reduce(f32[]{:T(128)} %multiply_reduce_fusion.1), channel_id=1, replica_groups=mesh['sector'=4,'op'=8] {'sector','op'}, use_global_device_ids=true, to_apply=%region_7.0 | all-reduce | flops 1 | bytes 8 | tf_op jit(solution)/shard_map/psum | solution.py:40
  455.7 0.8 multiply_reduce_fusion
  456.6 41.4 %psum.31 = f32[]{:T(128)} all-reduce(f32[]{:T(128)} %multiply_reduce_fusion), channel_id=1, replica_groups=mesh['sector'=4,'op'=8] {'sector','op'}, use_global_device_ids=true, to_apply=%region_9.0 | all-reduce | flops 1 | bytes 8 | tf_op jit(solution)/shard_map/psum | solution.py:42
  498.6 1.0 broadcast_multiply_fusion
  499.7 0.0 copy-done.3
  (2 shorter events, 0.0 us)
Async XLA Ops:
  7.2 85.1 %all-gather.3.cloned.1.call-start = ((), (), s32[]{:S(2)}) async-start(), calls=%async_computation.2 | async-start | bytes 5308416 | tf_op jit(solution)/shard_map/all_gather | solution.py:18
  7.9 138.1 %all-gather.5.cloned.1.call-start = ((), (), s32[]{:S(2)}) async-start(), calls=%async_computation.3 | async-start | bytes 2654208 | tf_op jit(solution)/shard_map/all_gather | solution.py:19
  8.9 6.7 %collective-permute-start = (f32[1,96,768]{2,1,0:T(8,128)S(1)}, f32[1,96,768]{2,1,0:T(8,128)S(1)}, u32[]{:S(2)}, u32[]{:S(2)}) collective-permute-start(f32[1,96,768]{2,1,0:T(8,128)S(1)} %slice.19), channel_id=1, source_target_pairs={{0,24},{8,0},{16,8},{24,16},{1,25},{9,1},{17,9},{25,17},{2,26},{10... | collective-permute-start | bytes 884744 | tf_op jit(solution)/shard_map/ppermute | solution.py:9
  15.6 0.7 copy-start.4
  16.4 256.0 %reduce-scatter.5.cloned.1.call-start = ((), (), s32[]{:S(2)}) async-start(), calls=%async_computation.5 | async-start | bytes 2654208 | tf_op jit(solution)/shard_map/reduce_scatter | solution.py:31
  92.3 2.3 copy-start.1
  92.3 28.7 %slice-start.3 = ((s8[9437184]{0:T(1024)(128)(4,1)}), s8[4194304]{0:T(1024)(128)(4,1)S(1)}, s32[]{:S(2)}) async-start(s8[9437184]{0:T(1024)(128)(4,1)} %bitcast.27), calls=%async_computation.9 | async-start | bytes 8388608
  94.6 26.4 %slice-start.4 = ((s8[9437184]{0:T(1024)(128)(4,1)}), s8[4194304]{0:T(1024)(128)(4,1)S(1)}, s32[]{:S(2)}) async-start(s8[9437184]{0:T(1024)(128)(4,1)} %bitcast.27), calls=%async_computation.10 | async-start | bytes 8388608
  94.6 26.4 %slice-start.5 = ((s8[9437184]{0:T(1024)(128)(4,1)}), s8[1048576]{0:T(1024)(128)(4,1)S(1)}, s32[]{:S(2)}) async-start(s8[9437184]{0:T(1024)(128)(4,1)} %bitcast.27), calls=%async_computation.11 | async-start | bytes 2097152
  121.0 24.9 %slice-start = ((f32[2,768,768]{2,1,0:T(8,128)}), f32[1,768,768]{2,1,0:T(8,128)S(1)}, s32[]{:S(2)}) async-start(f32[2,768,768]{2,1,0:T(8,128)} %all-gather.3.cloned.1.call-done), calls=%async_computation.6 | async-start | bytes 4718592 | tf_op jit(solution)/shard_map/slice | solution.py:21
  146.0 55.6 %slice-start.1 = ((s8[4718592]{0:T(1024)(128)(4,1)}), s8[4194304]{0:T(1024)(128)(4,1)S(1)}, s32[]{:S(2)}) async-start(s8[4718592]{0:T(1024)(128)(4,1)} %bitcast.25), calls=%async_computation.7 | async-start | bytes 8388608
  175.8 25.7 %slice-start.2 = ((s8[4718592]{0:T(1024)(128)(4,1)}), s8[524288]{0:T(1024)(128)(4,1)S(1)}, s32[]{:S(2)}) async-start(s8[4718592]{0:T(1024)(128)(4,1)} %bitcast.25), calls=%async_computation.8 | async-start | bytes 1048576
  204.4 166.4 %reduce-scatter.3.cloned.1.call-start = ((), (), s32[]{:S(2)}) async-start(), calls=%async_computation.4 | async-start | bytes 5308416 | tf_op jit(solution)/shard_map/reduce_scatter | solution.py:30
  208.5 162.3 %copy-start = (f32[2,96,768]{2,1,0:T(8,128)S(1)}, f32[2,96,768]{2,1,0:T(8,128)}, u32[]{:S(2)}) copy-start(f32[2,96,768]{2,1,0:T(8,128)} %param.5) | copy-start | bytes 1769476
  208.5 162.3 %copy-start.2 = (f32[2,96,768]{2,1,0:T(8,128)S(1)}, f32[2,96,768]{2,1,0:T(8,128)}, u32[]{:S(2)}) copy-start(f32[2,96,768]{2,1,0:T(8,128)} %param.6) | copy-start | bytes 1769476
  272.4 6.4 %collective-permute-start.1 = (f32[1,96,768]{2,1,0:T(8,128)}, f32[1,96,768]{2,1,0:T(8,128)S(1)}, u32[]{:S(2)}, u32[]{:S(2)}) collective-permute-start(f32[1,96,768]{2,1,0:T(8,128)} %reduce-scatter.5.cloned.1.call-done), channel_id=1, source_target_pairs={{0,8},{8,16},{16,24},{24,0},{1,9},{9,17},{17,25},{25,1},{2,10},{10... | collective-permute-start | bytes 884744 | tf_op jit(solution)/shard_map/ppermute | solution.py:9
  372.6 127.0 %copy-start.3 = (f32[2,96,768]{2,1,0:T(8,128)}, f32[2,96,768]{2,1,0:T(8,128)S(1)}, u32[]{:S(2)}) copy-start(f32[2,96,768]{2,1,0:T(8,128)S(1)} %get-tuple-element.6) | copy-start | bytes 1769476
Sparse Core Ops, SparseCore 0:
  10.2 82.0 all-gather.2
  95.0 50.1 all-gather.4
  204.5 67.8 reduce-scatter.4
  275.9 94.8 reduce-scatter.2
where the time goes:
time: 513 us; the launch traced here: 506 us
  waiting for transfers between devices  242 us (47%)
  blocking collectives  121 us (24%)
  matrix products  107 us (21%)
  between operations  17.4 us (3%)
  other arithmetic  12 us (2%)
    reduce_scatter x1, waiting for transfers between devices, on_device(): lax.psum_scatter(partial_sums, 'op', scatter_dimension=1, tiled=True)  92 us
    all_gather x1, waiting for transfers between devices, on_device(): lax.all_gather(wave, 'op', axis=1, tiled=True)  75.2 us
    reduce_scatter x1, waiting for transfers between devices, on_device(): lax.psum_scatter(leaving, 'op', scatter_dimension=1, tiled=True)  63.8 us
    psum x1, blocking collectives, on_device(): length_sq = lax.psum(jnp.sum(second * second), ('sector', 'op'))  41.4 us
    psum x1, blocking collectives, on_device(): lax.psum((jnp.sum(wave * wave), jnp.sum(wave * sigma)), ('sector', 'op'))  40.4 us
    psum x1, blocking collectives, on_device(): correlation = lax.psum(jnp.sum(wave * first), ('sector', 'op'))  39.3 us
    dot_general x1, matrix products, on_device(): jnp.einsum('jkca,jcb->jkab', left_ops, following, precision=highest)  29.8 us
    dot_general x1, matrix products, on_device(): jnp.einsum('jkac,jcb->jkab', left_ops, own_full, precision=highest)  26.4 us
  transfers between devices with their start and end apart: 6, of which 5 were waited for; matrix products, arithmetic and copies ran while one was open for 11% of the time, Pallas kernels for 0%

commit v1 on v0

--- a/solution.py
+++ b/solution.py
@@ -14,8 +14,31 @@
     rows = wave.shape[1]
     width = wave.shape[2]
     ahead_rows = shifted(wave[0:1], "sector", -1)
+
+    def wires_lay(chip_axis, mat):
+        t_next = lax.axis_index(chip_axis)
+        base_arr = lax.axis_size(chip_axis)
+        small, taken_in, moved = (base_arr, t_next, mat.shape[1])
+        sides = [(s, (s + 1) % small) for s in range(small)]
+        table = [(s, (s - 1) % small) for s in range(small)]
+        frame_out = jnp.zeros((*mat.shape[:1], small * moved, *mat.shape[2:]), mat.dtype)
+        frame_out = lax.dynamic_update_slice_in_dim(frame_out, mat, taken_in * moved, axis=1)
+        wide_out = small // 2
+        clean = reached = mat
+        for rr in range(1, wide_out + 1):
+            clean = lax.ppermute(clean, axis_name=chip_axis, perm=sides)
+            frame_out = lax.dynamic_update_slice_in_dim(
+                frame_out, clean, (taken_in - rr) % small * moved, axis=1
+            )
+            if rr < small - wide_out:
+                reached = lax.ppermute(reached, perm=table, axis_name=chip_axis)
+                frame_out = lax.dynamic_update_slice_in_dim(
+                    frame_out, reached, (taken_in + rr) % small * moved, axis=1
+                )
+        return frame_out
+
     own_full, ahead_full = (
-        lax.all_gather(wave, "op", axis=1, tiled=True),
+        wires_lay("op", wave),
         lax.all_gather(ahead_rows, "op", axis=1, tiled=True),
     )
     following = jnp.concatenate([own_full[1:2], ahead_full], axis=0)

time: 513 us -> 539 us (1.051)
  waiting for transfers between devices: 242 us -> 260 us
  starting transfers between devices: 2.62 us -> 13.8 us
    ppermute x0 -> x7, waiting for transfers between devices: none -> 97.2 us  [the longest x4 66.9 us: wires_lay(): clean = lax.ppermute(clean, axis_name=chip_axis, perm=sides)]
    all_gather x1 -> x0, waiting for transfers between devices: 75.2 us -> none  [on_device(): lax.all_gather(wave, 'op', axis=1, tiled=True)]
    ppermute x0 -> x7, starting transfers between devices: none -> 13 us  [the longest x4 7.91 us: wires_lay(): clean = lax.ppermute(clean, axis_name=chip_axis, perm=sides)]
  transfers between devices with their start and end apart: 6 -> 12, of which waited for: 5 -> 10; matrix products, arithmetic and copies ran while one was open for 11% -> 11% of each run, Pallas kernels for 0% -> 0%
where the time goes in v1:
time: 539 us; the launch traced here: 533 us
  waiting for transfers between devices  260 us (48%)
  blocking collectives  121 us (22%)
  matrix products  106 us (20%)
  between operations  17.6 us (3%)
  starting transfers between devices  13.8 us (3%)
  other arithmetic  12.2 us (2%)
    reduce_scatter x1, waiting for transfers between devices, on_device(): lax.psum_scatter(partial_sums, 'op', scatter_dimension=1, tiled=True)  92.2 us
    ppermute x4, waiting for transfers between devices, wires_lay(): clean = lax.ppermute(clean, axis_name=chip_axis, perm=sides)  66.9 us
    reduce_scatter x1, waiting for transfers between devices, on_device(): lax.psum_scatter(leaving, 'op', scatter_dimension=1, tiled=True)  63.1 us
    psum x1, blocking collectives, on_device(): length_sq = lax.psum(jnp.sum(second * second), ('sector', 'op'))  41.4 us
    psum x1, blocking collectives, on_device(): lax.psum((jnp.sum(wave * wave), jnp.sum(wave * sigma)), ('sector', 'op'))  40.4 us
    psum x1, blocking collectives, on_device(): correlation = lax.psum(jnp.sum(wave * first), ('sector', 'op'))  39.3 us
    ppermute x3, waiting for transfers between devices, wires_lay(): reached = lax.ppermute(reached, perm=table, axis_name=chip_axis)  30.3 us
    dot_general x1, matrix products, on_device(): jnp.einsum('jkca,jcb->jkab', left_ops, following, precision=highest)  29.8 us
  transfers between devices with their start and end apart: 12, of which 10 were waited for; matrix products, arithmetic and copies ran while one was open for 11% of the time, Pallas kernels for 0%

profile of v1, /device:TPU:0, one launch (start us, length us, event | category | flops | bytes accessed | tf_op | source)
XLA Modules:
  0.0 532.7 jit_solution(12677223844096899724)
XLA Ops:
  7.2 0.0 copy-start.1
  7.2 0.0 all-gather.2.cloned.1.call-start
  7.2 3.0 collective-permute-start
  10.3 1.0 slice.19
  11.3 0.7 collective-permute-start.7
  12.0 3.4 collective-permute-start.1
  15.4 0.9 collective-permute-done.7
  16.2 0.0 copy-start.4
  16.2 0.7 copy-done.4
  16.9 0.0 all-gather.2.cloned.1.call-update
  17.0 0.0 reduce-scatter.5.cloned.1.call-start
  17.0 22.0 %collective-permute-done = f32[2,96,768]{2,1,0:T(8,128)S(1)} collective-permute-done((f32[2,96,768]{2,1,0:T(8,128)}, f32[2,96,768]{2,1,0:T(8,128)S(1)}, u32[]{:S(2)}, u32[]{:S(2)}) %collective-permute-start) | collective-permute-done | bytes 589856 | tf_op jit(solution)/shard_map/ppermute | solution.py:29
  39.0 2.4 collective-permute-start.2
  41.3 1.3 collective-permute-done.1
  42.6 1.7 collective-permute-start.3
  44.4 34.0 %collective-permute-done.2 = f32[2,96,768]{2,1,0:T(8,128)S(1)} collective-permute-done((f32[2,96,768]{2,1,0:T(8,128)S(1)}, f32[2,96,768]{2,1,0:T(8,128)S(1)}, u32[]{:S(2)}, u32[]{:S(2)}) %collective-permute-start.2) | collective-permute-done | bytes 589856 | tf_op jit(solution)/shard_map/ppermute | solution.py:29
  78.4 2.5 collective-permute-start.4
  80.9 0.7 convert_element_type.3
  81.6 0.3 broadcast_in_dim.2
  81.9 0.0 copy-done.1
  81.9 8.8 %collective-permute-done.3 = f32[2,96,768]{2,1,0:T(8,128)S(1)} collective-permute-done((f32[2,96,768]{2,1,0:T(8,128)S(1)}, f32[2,96,768]{2,1,0:T(8,128)S(1)}, u32[]{:S(2)}, u32[]{:S(2)}) %collective-permute-start.3) | collective-permute-done | bytes 589856 | tf_op jit(solution)/shard_map/ppermute | solution.py:34
  90.8 0.0 collective-permute-start.5
  90.8 10.9 %collective-permute-done.4 = f32[2,96,768]{2,1,0:T(8,128)S(1)} collective-permute-done((f32[2,96,768]{2,1,0:T(8,128)S(1)}, f32[2,96,768]{2,1,0:T(8,128)S(1)}, u32[]{:S(2)}, u32[]{:S(2)}) %collective-permute-start.4) | collective-permute-done | bytes 589856 | tf_op jit(solution)/shard_map/ppermute | solution.py:29
  101.8 0.0 collective-permute-start.6
  101.9 0.0 copy-start
  102.0 20.2 %collective-permute-done.5 = f32[2,96,768]{2,1,0:T(8,128)S(1)} collective-permute-done((f32[2,96,768]{2,1,0:T(8,128)S(1)}, f32[2,96,768]{2,1,0:T(8,128)S(1)}, u32[]{:S(2)}, u32[]{:S(2)}) %collective-permute-start.5) | collective-permute-done | bytes 589856 | tf_op jit(solution)/shard_map/ppermute | solution.py:34
  122.2 0.0 collective-permute-done.6
  122.3 0.0 slice-start.2
  122.3 0.2 slice.24
  122.5 0.0 copy-done
  122.5 0.0 slice-start.3
  122.5 0.0 slice-start.4
  122.5 25.2 %fusion.9 = f32[2,768,2,768]{1,3,2,0:T(8,128)S(1)} fusion(f32[2,2,768,768]{3,2,1,0:T(8,128)S(1)} %copy-done, f32[2,768,768]{2,1,0:T(8,128)S(1)} %constant_dynamic-update-slice_fusion), kind=kOutput, calls=%fused_computation.11 | convolution fusion | flops 21743271936 | bytes 23592960 | tf_op jit(solution)/shard_map/jkac,jcb->jkab/dot_general | solution.py:45
  147.7 0.0 slice-done.2
  147.7 0.0 slice-done.3
  147.7 0.0 slice-done.4
  147.7 24.9 %fusion.16 = f32[2,768,768]{2,1,0:T(8,128)} fusion(f32[2,2,768,768]{3,2,1,0:T(8,128)S(1)} %bitcast.33, f32[2,768,2,768]{1,3,2,0:T(8,128)S(1)} %fusion.9, f32[2,2]{1,0:T(2,128)S(1)} %convert_element_type.3), kind=kOutput, calls=%fused_computation.17 | convolution fusion | flops 21745631232 | bytes 23592976 | tf_op jit(solution)/shard_map/jkab,jkcb->jac/dot_general | solution.py:48
  172.6 0.0 all-gather.2.cloned.1.call-done
  172.6 0.0 slice-start
  172.6 29.8 %fusion.6 = f32[2,768,2,768]{1,3,2,0:T(8,128)S(1)} fusion(f32[2,2,768,768]{3,2,1,0:T(8,128)} %param.7, f32[1,768,768]{2,1,0:T(8,128)} %all-gather.2.cloned.1.call-done, f32[1,768,768]{2,1,0:T(8,128)S(1)} %slice.24), kind=kOutput, calls=%fused_computation.7 | convolution fusion | flops 21744451584 | bytes 23592960 | tf_op jit(solution)/shard_map/jkca,jcb->jkab/dot_general | solution.py:46
  202.4 0.0 slice-start.1
  202.4 25.7 %fusion.13 = f32[2,768,768]{2,1,0:T(8,128)S(1)} fusion(f32[2,2,768,768]{3,2,1,0:T(8,128)} %param.8, f32[2,768,2,768]{1,3,2,0:T(8,128)S(1)} %fusion.6, f32[2,2]{1,0:T(2,128)S(1)} %convert_element_type.3), kind=kOutput, calls=%fused_computation.16 | convolution fusion | flops 21745631232 | bytes 23592976 | tf_op jit(solution)/shard_map/jkab,jkbc->jac/dot_general | solution.py:49
  228.1 0.0 slice-done
  228.1 0.0 slice-done.1
  228.2 2.8 fusion.20
  230.9 0.0 reduce-scatter.5.cloned.1.call-update
  231.0 0.0 reduce-scatter.3.cloned.1.call-start
  231.0 4.1 pad_maximum_fusion
  235.1 0.0 copy-start.2
  235.1 0.0 reduce-scatter.3.cloned.1.call-update
  235.1 63.1 %reduce-scatter.5.cloned.1.call-done = f32[1,96,768]{2,1,0:T(8,128)} async-done(((f32[1,768,768]{2,1,0:T(8,128)}), f32[1,96,768]{2,1,0:T(8,128)}) %reduce-scatter.5.cloned.1.call-update) | async-done | bytes 294928 | tf_op jit(solution)/shard_map/reduce_scatter | solution.py:54
  298.3 0.0 collective-permute-start.8
  298.3 6.4 %collective-permute-done.8 = f32[1,96,768]{2,1,0:T(8,128)S(1)} collective-permute-done((f32[1,96,768]{2,1,0:T(8,128)}, f32[1,96,768]{2,1,0:T(8,128)S(1)}, u32[]{:S(2)}, u32[]{:S(2)}) %collective-permute-start.8) | collective-permute-done | bytes 294944 | tf_op jit(solution)/shard_map/ppermute | solution.py:9
  304.6 92.2 %reduce-scatter.3.cloned.1.call-done = f32[2,96,768]{2,1,0:T(8,128)} async-done(((f32[2,768,768]{2,1,0:T(8,128)}), f32[2,96,768]{2,1,0:T(8,128)}) %reduce-scatter.3.cloned.1.call-update) | async-done | bytes 589840 | tf_op jit(solution)/shard_map/reduce_scatter | solution.py:53
  396.9 0.0 copy-done.2
  396.9 1.9 multiply_reduce_fusion.2
  398.8 0.0 copy-start.3
  398.8 40.4 %all-reduce.1 = (f32[]{:T(128)}, f32[]{:T(128)}) all-reduce(f32[]{:T(128)} %get-tuple-element.3, f32[]{:T(128)} %get-tuple-element.2), channel_id=1, replica_groups=mesh['sector'=4,'op'=8] {'sector','op'}, use_global_device_ids=true, to_apply=%region_3.4 | all-reduce | flops 2 | bytes 16 | tf_op jit(solution)/shard_map/psum | solution.py:59
  440.5 0.8 multiply_reduce_fusion.1
  441.4 39.3 %psum.30 = f32[]{:T(128)} all-reduce(f32[]{:T(128)} %multiply_reduce_fusion.1), channel_id=1, replica_groups=mesh['sector'=4,'op'=8] {'sector','op'}, use_global_device_ids=true, to_apply=%region_7.8 | all-reduce | flops 1 | bytes 8 | tf_op jit(solution)/shard_map/psum | solution.py:63
  482.0 0.8 multiply_reduce_fusion
  482.8 41.4 %psum.31 = f32[]{:T(128)} all-reduce(f32[]{:T(128)} %multiply_reduce_fusion), channel_id=1, replica_groups=mesh['sector'=4,'op'=8] {'sector','op'}, use_global_device_ids=true, to_apply=%region_9.10 | all-reduce | flops 1 | bytes 8 | tf_op jit(solution)/shard_map/psum | solution.py:65
  524.9 1.0 broadcast_multiply_fusion
  525.9 0.0 copy-done.3
  (10 shorter events, 0.4 us)
Async XLA Ops:
  7.2 74.7 %copy-start.1 = (f32[2,96,768]{2,1,0:T(8,128)S(1)}, f32[2,96,768]{2,1,0:T(8,128)}, u32[]{:S(2)}) copy-start(f32[2,96,768]{2,1,0:T(8,128)} %param.5) | copy-start | bytes 1769476
  7.2 165.4 %all-gather.2.cloned.1.call-start = ((), (), s32[]{:S(2)}) async-start(), calls=%async_computation.2 | async-start | bytes 2654208 | tf_op jit(solution)/shard_map/all_gather | solution.py:42
  7.2 31.8 %collective-permute-start = (f32[2,96,768]{2,1,0:T(8,128)}, f32[2,96,768]{2,1,0:T(8,128)S(1)}, u32[]{:S(2)}, u32[]{:S(2)}) collective-permute-start(f32[2,96,768]{2,1,0:T(8,128)} %param.5), channel_id=1, source_target_pairs={{0,1},{1,2},{2,3},{3,4},{4,5},{5,6},{6,7},{7,0},{8,9},{9,10},{10,1... | collective-permute-start | bytes 1769480 | tf_op jit(solution)/shard_map/ppermute | solution.py:29
  11.3 4.9 collective-permute-start.7
  12.0 30.7 %collective-permute-start.1 = (f32[2,96,768]{2,1,0:T(8,128)}, f32[2,96,768]{2,1,0:T(8,128)S(1)}, u32[]{:S(2)}, u32[]{:S(2)}) collective-permute-start(f32[2,96,768]{2,1,0:T(8,128)} %param.5), channel_id=1, source_target_pairs={{0,7},{1,0},{2,1},{3,2},{4,3},{5,4},{6,5},{7,6},{8,15},{9,8},{10,9... | collective-permute-start | bytes 1769480 | tf_op jit(solution)/shard_map/ppermute | solution.py:34
  16.2 0.7 copy-start.4
  17.0 281.3 %reduce-scatter.5.cloned.1.call-start = ((), (), s32[]{:S(2)}) async-start(), calls=%async_computation.4 | async-start | bytes 2654208 | tf_op jit(solution)/shard_map/reduce_scatter | solution.py:54
  39.0 39.4 %collective-permute-start.2 = (f32[2,96,768]{2,1,0:T(8,128)S(1)}, f32[2,96,768]{2,1,0:T(8,128)S(1)}, u32[]{:S(2)}, u32[]{:S(2)}) collective-permute-start(f32[2,96,768]{2,1,0:T(8,128)S(1)} %collective-permute-done), channel_id=1, source_target_pairs={{0,1},{1,2},{2,3},{3,4},{4,5},{5,6},{6,7},{7,0},{8,9},{9,10},{10,1... | collective-permute-start | bytes 1769480 | tf_op jit(solution)/shard_map/ppermute | solution.py:29
  42.6 48.1 %collective-permute-start.3 = (f32[2,96,768]{2,1,0:T(8,128)S(1)}, f32[2,96,768]{2,1,0:T(8,128)S(1)}, u32[]{:S(2)}, u32[]{:S(2)}) collective-permute-start(f32[2,96,768]{2,1,0:T(8,128)S(1)} %collective-permute-done.1), channel_id=1, source_target_pairs={{0,7},{1,0},{2,1},{3,2},{4,3},{5,4},{6,5},{7,6},{8,15},{9,8},{10,9... | collective-permute-start | bytes 1769480 | tf_op jit(solution)/shard_map/ppermute | solution.py:34
  78.4 23.4 %collective-permute-start.4 = (f32[2,96,768]{2,1,0:T(8,128)S(1)}, f32[2,96,768]{2,1,0:T(8,128)S(1)}, u32[]{:S(2)}, u32[]{:S(2)}) collective-permute-start(f32[2,96,768]{2,1,0:T(8,128)S(1)} %collective-permute-done.2), channel_id=1, source_target_pairs={{0,1},{1,2},{2,3},{3,4},{4,5},{5,6},{6,7},{7,0},{8,9},{9,10},{10,1... | collective-permute-start | bytes 1769480 | tf_op jit(solution)/shard_map/ppermute | solution.py:29
  90.8 31.4 %collective-permute-start.5 = (f32[2,96,768]{2,1,0:T(8,128)S(1)}, f32[2,96,768]{2,1,0:T(8,128)S(1)}, u32[]{:S(2)}, u32[]{:S(2)}) collective-permute-start(f32[2,96,768]{2,1,0:T(8,128)S(1)} %collective-permute-done.3), channel_id=1, source_target_pairs={{0,7},{1,0},{2,1},{3,2},{4,3},{5,4},{6,5},{7,6},{8,15},{9,8},{10,9... | collective-permute-start | bytes 1769480 | tf_op jit(solution)/shard_map/ppermute | solution.py:34
  101.8 20.4 %collective-permute-start.6 = (f32[2,96,768]{2,1,0:T(8,128)S(1)}, f32[2,96,768]{2,1,0:T(8,128)S(1)}, u32[]{:S(2)}, u32[]{:S(2)}) collective-permute-start(f32[2,96,768]{2,1,0:T(8,128)S(1)} %collective-permute-done.4), channel_id=1, source_target_pairs={{0,1},{1,2},{2,3},{3,4},{4,5},{5,6},{6,7},{7,0},{8,9},{9,10},{10,1... | collective-permute-start | bytes 1769480 | tf_op jit(solution)/shard_map/ppermute | solution.py:29
  101.9 20.6 %copy-start = (f32[2,2,768,768]{3,2,1,0:T(8,128)S(1)}, f32[2,2,768,768]{3,2,1,0:T(8,128)}, u32[]{:S(2)}) copy-start(f32[2,2,768,768]{3,2,1,0:T(8,128)} %param.7) | copy-start | bytes 28311556
  122.3 25.4 %slice-start.2 = ((s8[9437184]{0:T(1024)(128)(4,1)}), s8[4194304]{0:T(1024)(128)(4,1)S(1)}, s32[]{:S(2)}) async-start(s8[9437184]{0:T(1024)(128)(4,1)} %bitcast.32), calls=%async_computation.7 | async-start | bytes 8388608
  122.5 25.2 %slice-start.3 = ((s8[9437184]{0:T(1024)(128)(4,1)}), s8[4194304]{0:T(1024)(128)(4,1)S(1)}, s32[]{:S(2)}) async-start(s8[9437184]{0:T(1024)(128)(4,1)} %bitcast.32), calls=%async_computation.8 | async-start | bytes 8388608
  122.5 25.2 %slice-start.4 = ((s8[9437184]{0:T(1024)(128)(4,1)}), s8[1048576]{0:T(1024)(128)(4,1)S(1)}, s32[]{:S(2)}) async-start(s8[9437184]{0:T(1024)(128)(4,1)} %bitcast.32), calls=%async_computation.9 | async-start | bytes 2097152
  172.6 55.5 %slice-start = ((s8[4718592]{0:T(1024)(128)(4,1)}), s8[4194304]{0:T(1024)(128)(4,1)S(1)}, s32[]{:S(2)}) async-start(s8[4718592]{0:T(1024)(128)(4,1)} %bitcast.30), calls=%async_computation.5 | async-start | bytes 8388608
  202.4 25.7 %slice-start.1 = ((s8[4718592]{0:T(1024)(128)(4,1)}), s8[524288]{0:T(1024)(128)(4,1)S(1)}, s32[]{:S(2)}) async-start(s8[4718592]{0:T(1024)(128)(4,1)} %bitcast.30), calls=%async_computation.6 | async-start | bytes 1048576
  231.0 165.9 %reduce-scatter.3.cloned.1.call-start = ((), (), s32[]{:S(2)}) async-start(), calls=%async_computation.3 | async-start | bytes 5308416 | tf_op jit(solution)/shard_map/reduce_scatter | solution.py:53
  235.1 161.8 %copy-start.2 = (f32[2,96,768]{2,1,0:T(8,128)S(1)}, f32[2,96,768]{2,1,0:T(8,128)}, u32[]{:S(2)}) copy-start(f32[2,96,768]{2,1,0:T(8,128)} %param.6) | copy-start | bytes 1769476
  298.3 6.4 %collective-permute-start.8 = (f32[1,96,768]{2,1,0:T(8,128)}, f32[1,96,768]{2,1,0:T(8,128)S(1)}, u32[]{:S(2)}, u32[]{:S(2)}) collective-permute-start(f32[1,96,768]{2,1,0:T(8,128)} %reduce-scatter.5.cloned.1.call-done), channel_id=1, source_target_pairs={{0,8},{8,16},{16,24},{24,0},{1,9},{9,17},{17,25},{25,1},{2,10},{10... | collective-permute-start | bytes 884744 | tf_op jit(solution)/shard_map/ppermute | solution.py:9
  398.8 127.2 %copy-start.3 = (f32[2,96,768]{2,1,0:T(8,128)}, f32[2,96,768]{2,1,0:T(8,128)S(1)}, u32[]{:S(2)}) copy-start(f32[2,96,768]{2,1,0:T(8,128)S(1)} %get-tuple-element.6) | copy-start | bytes 1769476
Sparse Core Ops, SparseCore 0:
  17.1 87.5 all-gather.1
  231.1 67.1 reduce-scatter.4
  301.9 94.9 reduce-scatter.2
